TPU v7x, 32 devices: a whole 2x2x4 slice. The times are simulated.
32 devices in a mesh: group: 4 (over z), dev: 8 (over y, x, core).
Axes of the slice: x: 2, y: 2, z: 4, core: 2. Of those that a mesh axis runs over, the one named last changes fastest.
Arguments:
- tile_values: bfloat16 [512, 128, 128], P(('group', 'dev')), may hold values from -0.25 to 0.25
- tile_rows: int32 [512], P(('group', 'dev')), may hold values from 0 to 1
- tile_columns: int32 [512], P(('group', 'dev')), may hold values from 0 to 15
- tile_count: int32 [32], P(('group', 'dev')), may hold values from 4 to 16, as said below
- start_basis: bfloat16 [8192, 64], P(('group', 'dev')), may hold values from -6 to 6
- seed_rows: int32 [1024], replicated, may hold values from 0 to 8191
Outputs:
- unit_embedding: float32 [8192, 64], P(('group', 'dev'))
- centroids: float32 [1024, 64], replicated
Inputs may be any that keep to these rules, and one draw needn't show every extreme that they name: `tile_count`: the most, 16, is reached by some device in every draw.
All inputs are finite; a program needn't handle non-finite values.
Results may differ from a plain program's by a relative error of at most 0.0029.
Values may be sent and summed in bfloat16 or wider, within the bound.
A program may use at most 64 MiB of HBM per device.

v0:
```python
import functools

import jax
import jax.numpy as jnp
from jax import lax
from jax.experimental import pallas as pl
from jax.experimental.pallas import tpu as pltpu
from jax.sharding import PartitionSpec as P

KSTEPS = 2
SHARPNESS = 4.0
MASS_ROWS = 16
MESH = pl.DeviceIdType.MESH
F32 = jnp.float32
HIGHEST = lax.Precision.HIGHEST
NN = (((1,), (0,)), ((), ()))
NT = (((1,), (1,)), ((), ()))


def mm(a, b, dims=NN):
    return lax.dot_general(a, b, dims, precision=HIGHEST, preferred_element_type=F32)


def high_low(x):
    high = x.astype(jnp.bfloat16)
    return high, (x - high.astype(F32)).astype(jnp.bfloat16)


def dot16(a, b):
    return lax.dot_general(a, b, NN, preferred_element_type=F32)


def loop(n, body):
    if n <= 8:
        for i in range(n):
            body(i)
    else:

        def step(i, carry):
            body(i)
            return carry

        lax.fori_loop(0, n, step, 0)


def fold(n, ref):
    total = ref[0].astype(F32)
    if n <= 8:
        for i in range(1, n):
            total = total + ref[i].astype(F32)
        return total
    return lax.fori_loop(1, n, lambda i, total: total + ref[i].astype(F32), total)


class Exchange:
    def __init__(self, axis, n, me, land, sems, source=None):
        self.axis, self.n, self.me = axis, n, me
        self.land, self.source = land, source
        self.send, self.recv = sems

    def copy(self, peer, slot):
        source = self.land(self.me) if self.source is None else self.source(peer)
        return pltpu.make_async_remote_copy(
            src_ref=source,
            dst_ref=self.land(slot),
            send_sem=self.send.at[peer],
            recv_sem=self.recv.at[slot],
            device_id={self.axis: peer},
            device_id_type=MESH,
        )

    def peer(self, i):
        return lax.rem(self.me + 1 + i, self.n)

    def start(self):
        loop(self.n - 1, lambda i: self.copy(self.peer(i), self.me).start())

    def wait_recv(self):
        loop(self.n - 1, lambda i: self.copy(self.peer(i), self.peer(i)).wait_recv())

    def wait_send(self):
        loop(self.n - 1, lambda i: self.copy(self.peer(i), self.me).wait_send())


def factor_inverse(gram):
    k = gram.shape[0]
    rows = lax.broadcasted_iota(jnp.int32, (k, k), 0)
    lanes = lax.broadcasted_iota(jnp.int32, (k, k), 1)
    table = jnp.concatenate([gram, jnp.where(rows == lanes, 1.0, 0.0).astype(F32)], axis=1)
    parts = [table[8 * b : 8 * b + 8] for b in range(k // 8)]
    sub = lax.broadcasted_iota(jnp.int32, (8, 2 * k), 0)
    for i in range(0, k, 2):
        b, r = divmod(i, 8)
        own = parts[b]
        top, low = own[r : r + 1], own[r + 1 : r + 2]
        pivot, cross, corner = (
            jnp.broadcast_to(v, (1, 2 * k))
            for v in (top[:, i : i + 1], top[:, i + 1 : i + 2], low[:, i + 1 : i + 2])
        )
        over = 1.0 / pivot
        ratio = cross * over
        scaled_low = (low - ratio * top) / (corner - ratio * cross)
        scaled_top = (top - cross * scaled_low) * over

        def minus(part):
            return part - part[:, i : i + 1] * scaled_top - part[:, i + 1 : i + 2] * scaled_low

        fixed = jnp.where(sub == r + 1, own - ratio * top, own)
        parts[b] = jnp.where(sub > r + 1, minus(own), fixed) if r < 6 else fixed
        for c in range(b + 1, k // 8):
            parts[c] = minus(parts[c])
    table = jnp.concatenate(parts, axis=0)
    diag = jnp.sum(jnp.where(rows == lanes, table[:, :k], 0.0), axis=1, keepdims=True)
    return table[:, k:] / jnp.sqrt(diag)


def pack(gram):
    half = gram.shape[0] // 2
    return jnp.concatenate([gram[:half], gram[half:]], axis=1)


def unpack(packed):
    k = packed.shape[1] // 2
    return jnp.concatenate([packed[:, :k], packed[:, k:]], axis=0)


def kernel(
    n, m, total_rows,
    tiles, rows_ref, columns_ref, count_ref, start, seeds,
    unit_out, centres_out,
    matrix, basis0, basis1, images, gram_dev, gram_group,
    seed_out, seed_dev, seed_group, seed_all,
    *rest,
):
    me, g = lax.axis_index("dev"), lax.axis_index("group")
    k_out, k_dev, k_group, k_all, k_early = (rest[2 * i : 2 * i + 2] for i in range(5))
    sems = rest[10:]
    pairs = [(sems[2 * i], sems[2 * i + 1]) for i in range(len(sems) // 2)]
    slots, block = tiles.shape[0], tiles.shape[1]
    width, local_rows = start.shape
    row_blocks = local_rows // block
    clusters = seeds.shape[1]
    part = clusters // n

    barrier = pltpu.get_barrier_semaphore()
    for axis, size, index in (("dev", n, me), ("group", m, g)):
        loop(
            size - 1,
            lambda i: pl.semaphore_signal(
                barrier, inc=1, device_id={axis: lax.rem(index + 1 + i, size)}, device_id_type=MESH
            ),
        )
    for r in range(row_blocks):
        basis0[me * row_blocks + r] = start[:, r * block : (r + 1) * block]
    pl.semaphore_wait(barrier, n - 1 + m - 1)

    used = iter(pairs)
    pending = []

    def exchange(axis, land, source=None):
        size, index = (n, me) if axis == "dev" else (m, g)
        made = Exchange(axis, size, index, land, next(used), source)
        made.start()
        pending.append(made)
        return made

    own_blocks = lambda d: basis0.at[pl.ds(d * row_blocks, row_blocks)]
    gather = exchange("dev", own_blocks)
    count = count_ref[0]
    for s in range(slots):
        for r in range(row_blocks):
            keep = jnp.logical_and(rows_ref[s] == r, s < count)
            matrix[r * block : (r + 1) * block, s * block : (s + 1) * block] = tiles[s] * jnp.where(
                keep, 1.0, 0.0
            ).astype(jnp.bfloat16)

    def apply(basis):
        picked = jnp.concatenate([basis[columns_ref[s]] for s in range(slots)], axis=1)
        return lax.dot_general(picked, matrix[...], NT, preferred_element_type=F32)

    def start_gram(image, turn):
        gram_dev[turn, me] = pack(mm(image, image, NT))
        return exchange("dev", lambda d: gram_dev.at[turn, d])

    def end_gram(first, turn):
        first.wait_recv()
        gram_group[turn, g] = fold(n, gram_dev.at[turn])
        return exchange("group", lambda d: gram_group.at[turn, d])

    gather.wait_recv()
    image = apply(basis0)
    first = start_gram(image, 0)
    images[me] = image
    gather = exchange("dev", lambda d: images.at[d])
    second = end_gram(first, 0)
    second.wait_recv()
    inverse = factor_inverse(unpack(fold(m, gram_group.at[0])))
    gather.wait_recv()

    def solve(d):
        solved = mm(inverse, images[d])
        for r in range(row_blocks):
            basis1[d * row_blocks + r] = solved[:, r * block : (r + 1) * block].astype(jnp.bfloat16)

    loop(n, solve)
    image = apply(basis1)
    first = start_gram(image, 1)

    half = width // 2

    def split(values, out, extra=None):
        for h in range(2):
            for c in range(n):
                lanes = slice(c * part, (c + 1) * part)
                out[h][c, :half] = values[h * half : (h + 1) * half, lanes].astype(out[h].dtype)
                if h == 0 and extra is not None:
                    out[h][c, half:] = jnp.broadcast_to(
                        extra[:, lanes], (MASS_ROWS, part)
                    ).astype(out[h].dtype)

    def join(refs):
        return jnp.concatenate(
            [jnp.concatenate([ref[c] for c in range(n)], axis=1) for ref in refs], axis=0
        )

    def start_dev(out, dev):
        made = []
        for h in range(2):
            dev[h][me] = out[h][me]
            made.append(
                exchange("dev", lambda d, h=h: dev[h].at[d], lambda p, h=h: out[h].at[p])
            )
        return made

    def start_group(made, dev, group):
        after = []
        for h in range(2):
            made[h].wait_recv()
            total = fold(n, dev[h])
            group[h][g] = total[: group[h].shape[1]].astype(group[h].dtype)
            after.append(exchange("group", lambda d, h=h: group[h].at[d]))
        return after

    def start_all(made, group, every, finish):
        after = []
        for h in range(2):
            made[h].wait_recv()
            every[h][me] = finish(h, fold(m, group[h]))
            after.append(exchange("dev", lambda d, h=h: every[h].at[d]))
        return after

    first_row = (g * n + me) * local_rows
    chooser = jnp.where(
        lax.broadcasted_iota(jnp.int32, (local_rows, clusters), 0) == seeds[...] - first_row, 1.0, 0.0
    ).astype(jnp.bfloat16)
    high = image.astype(jnp.bfloat16)
    rest_of = image - high.astype(F32)
    pieces = dot16(jnp.concatenate([high, *high_low(rest_of)], axis=0), chooser)
    seed_out, seed_dev, seed_group, seed_all = (
        [ref.at[h] for h in range(2)] for ref in (seed_out, seed_dev, seed_group, seed_all)
    )
    split(pieces[:width] + pieces[width : 2 * width] + pieces[2 * width :], seed_out)
    made = start_dev(seed_out, seed_dev)
    second = end_gram(first, 1)
    made = start_group(made, seed_dev, seed_group)
    second.wait_recv()
    inverse = factor_inverse(unpack(fold(m, gram_group.at[1])))
    made = start_all(made, seed_group, seed_all, lambda h, total: total)

    def normalise(image_t):
        embedding = mm(inverse, image_t) * jnp.sqrt(F32(total_rows))
        return embedding / jnp.sqrt(jnp.sum(embedding * embedding, axis=0, keepdims=True) + 1e-06)

    unit_t = normalise(image)
    unit_out[...] = unit_t
    unit = unit_t.T
    unit_square = jnp.sum(unit * unit, axis=1, keepdims=True)
    unit_high, unit_low = high_low(unit_t)
    left = jnp.concatenate([unit_high, unit_low, unit_high], axis=0).astype(F32).T.astype(jnp.bfloat16)
    unit_pair = jnp.concatenate([unit_high, unit_low], axis=0)
    for gather in made:
        gather.wait_recv()
    centres = normalise(join(seed_all))
    for turn in range(KSTEPS):
        high, low = high_low(centres)
        inner = dot16(left, jnp.concatenate([high, high, low], axis=0))
        dist = unit_square - 2.0 * inner + jnp.sum(centres * centres, axis=0, keepdims=True)
        weights = jnp.exp(-SHARPNESS * dist)
        member = weights / jnp.sum(weights, axis=1, keepdims=True)
        out, dev, group, every = (
            [ref.at[turn] for ref in refs]
            for refs in (k_out, k_dev, k_group if turn + 1 == KSTEPS else k_early, k_all)
        )
        high, low = high_low(member)
        pair = dot16(unit_pair, high)
        split(pair[:width] + pair[width:] + dot16(unit_high, low), out, jnp.sum(member, axis=0, keepdims=True))
        made = start_group(start_dev(out, dev), dev, group)
        mass = []

        def finish(h, total):
            if h == 0:
                mass.append(total[half : half + 1])
            return total[:half] / mass[0]

        for gather in start_all(made, group, every, finish):
            gather.wait_recv()
        centres = join(every)
    centres_out[...] = centres
    for made in pending:
        made.wait_send()


def local(tile_values, tile_rows, tile_columns, tile_count, start_basis, seed_rows):
    n, m = lax.axis_size("dev"), lax.axis_size("group")
    slots, block = tile_values.shape[0], tile_values.shape[1]
    local_rows, width = start_basis.shape
    row_blocks = local_rows // block
    clusters = seed_rows.shape[0]
    part = clusters // n
    vmem = pl.BlockSpec(memory_space=pltpu.VMEM)
    smem = pl.BlockSpec(memory_space=pltpu.SMEM)
    half = (width // 2, 2 * width)
    axes = ["dev", "dev", "dev", "group", "dev", "dev", "dev", "group", "group", "group", "dev", "dev"]
    axes += ["dev", "dev", "group", "group", "dev", "dev"] * KSTEPS
    sems = []
    for axis in axes:
        sems += [pltpu.SemaphoreType.DMA((n if axis == "dev" else m,))] * 2
    unit, centres = pl.pallas_call(
        functools.partial(kernel, n, m, local_rows * n * m),
        out_shape=(
            jax.ShapeDtypeStruct((width, local_rows), F32),
            jax.ShapeDtypeStruct((width, clusters), F32),
        ),
        in_specs=[vmem, smem, smem, smem, vmem, vmem],
        out_specs=(vmem, vmem),
        scratch_shapes=[
            pltpu.VMEM((local_rows, slots * block), jnp.bfloat16),
            pltpu.VMEM((n * row_blocks, width, block), jnp.bfloat16),
            pltpu.VMEM((n * row_blocks, width, block), jnp.bfloat16),
            pltpu.VMEM((n, width, local_rows), F32),
            pltpu.VMEM((2, n, *half), F32),
            pltpu.VMEM((2, m, *half), F32),
            *[pltpu.VMEM((2, size, width // 2, part), F32) for size in (n, n, m, n)],
            *[
                pltpu.VMEM((KSTEPS, size, width // 2 + more, part), kind)
                for size, extra, kind in (
                    (n, MASS_ROWS, jnp.bfloat16),
                    (n, MASS_ROWS, jnp.bfloat16),
                    (m, 8, F32),
                    (n, 0, F32),
                    (m, MASS_ROWS, jnp.bfloat16),
                )
                for more in (extra, 0)
            ],
            *sems,
        ],
        compiler_params=pltpu.CompilerParams(
            collective_id=0, has_side_effects=True, vmem_limit_bytes=58 * 1024 * 1024
        ),
        name="spectral",
    )(tile_values, tile_rows, tile_columns, tile_count, start_basis.T, seed_rows[None, :])
    return unit.T, centres.T


def solution(mesh):
    return jax.shard_map(
        local,
        mesh=mesh,
        in_specs=(
            P(("group", "dev"), None, None),
            P(("group", "dev")),
            P(("group", "dev")),
            P(("group", "dev")),
            P(("group", "dev"), None),
            P(),
        ),
        out_specs=(P(("group", "dev"), None), P()),
        check_vma=False,
    )
```

profile of v0, /device:TPU:0, one launch (start us, length us, event | category | flops | bytes accessed | tf_op | source)
XLA Modules:
  0.0 75.0 jit_solution(17979005819687735423)
XLA Ops:
  1.3 70.6 %spectral.1 = (f32[64,256]{1,0:T(8,128)}, f32[64,1024]{1,0:T(8,128)}) custom-call(bf16[16,128,128]{2,1,0:T(8,128)(2,1)} %tiles.1, s32[16]{0:T(128)} %rows_ref.1, s32[16]{0:T(128)} %columns_ref.1, s32[1]{0:T(128)S(6)} %copy.10.count_ref, bf16[64,256]{1,0:T(8,128)(2,1)} %bitcast.6, s32[1,1024]{1,0:T(1,128)} %bitcast.7), custom_call_target="tpu_custom_call" | custom-call | tf_op jit(solution)/shard_map/spectral/pallas_call | solution.py:328
  71.9 1.5 %copy.11 = f32[256,64]{0,1:T(8,128)} copy(f32[256,64]{0,1:T(8,128)} %bitcast.5) | data formatting | bytes 131072
  73.3 1.7 %copy.12 = f32[1024,64]{0,1:T(8,128)} copy(f32[1024,64]{0,1:T(8,128)} %bitcast.4) | data formatting | bytes 524288
where the time goes:
time: 75.2 us; the launch traced here: 75 us
  Pallas kernels  70.6 us (94%)
  local copies, waits for them, and re-layouts  3.14 us (4%)
  between operations  1.29 us (2%)
    pallas_call x1, Pallas kernels, local(): pl.pallas_call(functools.partial(kernel, n, m, local_rows * n * m), out_s...  70.6 us
    unnamed x2, local copies, waits for them, and re-layouts  3.14 us

commit v1 on v0

v1 whole, which is shorter than its diff:
```python
import functools

import jax
import jax.numpy as jnp
from jax import lax
from jax.experimental import pallas as pl
from jax.experimental.pallas import tpu as pltpu
from jax.sharding import PartitionSpec as P

KSTEPS = 2
SHARPNESS = 4.0
MASS_ROWS = 16
LANES = 128
MESH = pl.DeviceIdType.MESH
F32 = jnp.float32
HIGHEST = lax.Precision.HIGHEST
NN = (((1,), (0,)), ((), ()))
NT = (((1,), (1,)), ((), ()))
TN = (((0,), (0,)), ((), ()))


def mm(a, b, dims=NN):
    return lax.dot_general(a, b, dims, precision=HIGHEST, preferred_element_type=F32)


def high_low(x):
    high = x.astype(jnp.bfloat16)
    return high, (x - high.astype(F32)).astype(jnp.bfloat16)


def dot16(a, b, dims=NN):
    return lax.dot_general(a, b, dims, preferred_element_type=F32)


def three(x):
    high = x.astype(jnp.bfloat16)
    return (high, *high_low(x - high.astype(F32)))


def loop(n, body):
    if n <= 8:
        for i in range(n):
            body(i)
    else:

        def step(i, carry):
            body(i)
            return carry

        lax.fori_loop(0, n, step, 0)


def fold(n, ref):
    total = ref[0].astype(F32)
    if n <= 8:
        for i in range(1, n):
            total = total + ref[i].astype(F32)
        return total
    return lax.fori_loop(1, n, lambda i, total: total + ref[i].astype(F32), total)


class Exchange:
    def __init__(self, axis, n, me, land, sems, source=None):
        self.axis, self.n, self.me = axis, n, me
        self.land, self.source = land, source
        self.send, self.recv = sems

    def copy(self, peer, slot):
        source = self.land(self.me) if self.source is None else self.source(peer)
        return pltpu.make_async_remote_copy(
            src_ref=source,
            dst_ref=self.land(slot),
            send_sem=self.send.at[peer],
            recv_sem=self.recv.at[slot],
            device_id={self.axis: peer},
            device_id_type=MESH,
        )

    def peer(self, i):
        return lax.rem(self.me + 1 + i, self.n)

    def start(self):
        loop(self.n - 1, lambda i: self.copy(self.peer(i), self.me).start())

    def wait_recv(self):
        loop(self.n - 1, lambda i: self.copy(self.peer(i), self.peer(i)).wait_recv())

    def wait_send(self):
        loop(self.n - 1, lambda i: self.copy(self.peer(i), self.me).wait_send())


def total_of(n, value):
    total = value(0)
    if n <= 8:
        for d in range(1, n):
            total = total + value(d)
        return total
    return lax.fori_loop(1, n, lambda d, total: total + value(d), total)


class Gather:
    def __init__(self, n, me, land, pairs):
        self.n, self.me, self.land = n, me, land
        self.pairs = pairs
        self.twin = self.me + 1 - 2 * lax.rem(self.me, 2)

    def copy(self, owner, slot, to, stage):
        send, recv = self.pairs[stage]
        return pltpu.make_async_remote_copy(
            src_ref=self.land(owner),
            dst_ref=self.land(owner),
            send_sem=send.at[slot],
            recv_sem=recv.at[owner],
            device_id={"dev": to},
            device_id_type=MESH,
        )

    def far(self, i):
        return lax.rem(self.me + 2 + 2 * i, self.n)

    def start(self):
        self.copy(self.me, self.me, self.twin, 1).start()
        loop(self.n // 2 - 1, lambda i: self.copy(self.me, self.far(i), self.far(i), 0).start())

    def relay(self):
        def one(i):
            owner = self.far(i)
            self.copy(owner, owner, owner, 0).wait_recv()
            self.copy(owner, owner, self.twin, 1).start()

        loop(self.n // 2 - 1, one)

    def other(self, i):
        return lax.rem(self.twin + 2 * i, self.n)

    def wait_recv(self):
        loop(self.n // 2, lambda i: self.copy(self.other(i), self.other(i), self.twin, 1).wait_recv())

    def wait_send(self):
        self.copy(self.me, self.me, self.twin, 1).wait_send()

        def one(i):
            owner = self.far(i)
            self.copy(self.me, owner, owner, 0).wait_send()
            self.copy(owner, owner, self.twin, 1).wait_send()

        loop(self.n // 2 - 1, one)


def factor_inverse(gram):
    k = gram.shape[0]
    wide = 2 * k
    rows = lax.broadcasted_iota(jnp.int32, (k, k), 0)
    lanes = lax.broadcasted_iota(jnp.int32, (k, k), 1)
    table = jnp.concatenate([gram, jnp.where(rows == lanes, 1.0, 0.0).astype(F32)], axis=1)
    count = k // 8
    parts = [table[8 * b : 8 * b + 8] for b in range(count)]
    sub = lax.broadcasted_iota(jnp.int32, (8, wide), 0)

    def full(v):
        return jnp.broadcast_to(v, (8, wide))

    done = []
    for b in range(count):
        own, at = parts[b], 8 * b
        row = [full(own[s : s + 1]) for s in range(8)]
        cell = [[full(own[s : s + 1, at + r : at + r + 1]) for r in range(s + 1)] for s in range(8)]
        column = {c: [full(parts[c][:, at + r : at + r + 1]) for r in range(8)] for c in range(b + 1, count)}
        over = []
        for r in range(8):
            over.append(1.0 / cell[r][r])
            for s in range(r + 1, 8):
                ratio = cell[s][r] * over[r]
                for t in range(r + 1, s + 1):
                    cell[s][t] = cell[s][t] - ratio * cell[t][r]
                row[s] = row[s] - ratio * row[r]
                for values in column.values():
                    values[s] = values[s] - ratio * values[r]
        for c, values in column.items():
            for r in range(8):
                parts[c] = parts[c] - values[r] * (row[r] * over[r])
        own = row[0] / jnp.sqrt(cell[0][0])
        for s in range(1, 8):
            own = jnp.where(sub == s, row[s] / jnp.sqrt(cell[s][s]), own)
        done.append(own)
    return jnp.concatenate(done, axis=0)[:, k:]


def pack(gram):
    half = gram.shape[0] // 2
    return jnp.concatenate([gram[:half], gram[half:]], axis=1)


def unpack(packed):
    k = packed.shape[1] // 2
    return jnp.concatenate([packed[:, :k], packed[:, k:]], axis=0)


def kernel(
    n, m, total_rows,
    tiles_in, rows_in, columns_in, count_in, start_in, seeds_in,
    unit_out, centres_out,
    tiles, rows_ref, columns_ref, count_ref, seeds,
    matrix, basis0, basis1, images0, images1, gram_dev, gram_group,
    chooser, seed_group, right, left, square, units, weights, den, weights_scale, sums, final,
    in_sems, out_sems, *sems,
):
    me, g = lax.axis_index("dev"), lax.axis_index("group")
    pairs = [(sems[2 * i], sems[2 * i + 1]) for i in range(len(sems) // 2)]
    slots, block = tiles.shape[0], tiles.shape[1]
    width, local_rows = start_in.shape
    row_blocks = local_rows // block
    part = seeds.shape[1]

    barrier = pltpu.get_barrier_semaphore()
    for axis, size, index in (("dev", n, me), ("group", m, g)):
        loop(
            size - 1,
            lambda i: pl.semaphore_signal(
                barrier, inc=1, device_id={axis: lax.rem(index + 1 + i, size)}, device_id_type=MESH
            ),
        )
    loads = [(start_in.at[:, r * block : (r + 1) * block], basis0.at[me * row_blocks + r]) for r in range(row_blocks)]
    loads += [(rows_in, rows_ref), (columns_in, columns_ref), (count_in, count_ref), (seeds_in.at[me], seeds)]
    loads += [(tiles_in, tiles)]
    loads = [pltpu.make_async_copy(a, b, in_sems.at[i]) for i, (a, b) in enumerate(loads)]
    for load in loads:
        load.start()
    for load in loads:
        load.wait()
    pl.semaphore_wait(barrier, n - 1 + m - 1)

    used = iter(pairs)
    pending = []

    def exchange(axis, land, source=None):
        size, index = (n, me) if axis == "dev" else (m, g)
        made = Exchange(axis, size, index, land, next(used), source)
        made.start()
        pending.append(made)
        return made

    gather = exchange("dev", lambda d: basis0.at[pl.ds(d * row_blocks, row_blocks)])
    count = count_ref[0, 0]
    for s in range(slots):
        for r in range(row_blocks):
            keep = jnp.logical_and(rows_ref[s] == r, s < count)
            matrix[r * block : (r + 1) * block, s * block : (s + 1) * block] = tiles[s] * jnp.where(
                keep, 1.0, 0.0
            ).astype(jnp.bfloat16)

    def choose(d):
        first_row = (g * n + d) * local_rows
        chooser[d] = jnp.where(
            lax.broadcasted_iota(jnp.int32, (local_rows, part), 0) == seeds[...] - first_row, 1.0, 0.0
        ).astype(jnp.bfloat16)
        right[d, 3 * width :] = jnp.ones((MASS_ROWS, local_rows), jnp.bfloat16)
        left[d, 2 * width :] = jnp.ones((MASS_ROWS, local_rows), jnp.bfloat16)

    loop(n, choose)

    def apply(basis):
        picked = jnp.concatenate([basis[columns_ref[s]] for s in range(slots)], axis=1)
        return lax.dot_general(picked, matrix[...], NT, preferred_element_type=F32)

    def start_gram(image, turn):
        gram_dev[turn, me] = pack(mm(image, image, NT))
        return exchange("dev", lambda d: gram_dev.at[turn, d])

    def end_gram(first, turn):
        first.wait_recv()
        gram_group[turn, g] = fold(n, gram_dev.at[turn])
        return exchange("group", lambda d: gram_group.at[turn, d])

    gather.wait_recv()
    image = apply(basis0)
    first = start_gram(image, 0)
    images0[me] = image
    gather = exchange("dev", lambda d: images0.at[d])
    second = end_gram(first, 0)
    second.wait_recv()
    inverse = factor_inverse(unpack(fold(m, gram_group.at[0])))
    gather.wait_recv()

    def solve(d):
        solved = mm(inverse, images0[d])
        for r in range(row_blocks):
            basis1[d * row_blocks + r] = solved[:, r * block : (r + 1) * block].astype(jnp.bfloat16)

    loop(n, solve)
    image = apply(basis1)
    first = start_gram(image, 1)
    images1[me] = image
    gather = Gather(n, me, lambda d: images1.at[d], [next(used) for _ in range(2)])
    gather.start()
    second = end_gram(first, 1)
    gather.relay()
    gather.wait_recv()

    def chosen(d):
        pieces = dot16(jnp.concatenate(three(images1[d]), axis=0), chooser[d])
        return pieces[:width] + pieces[width : 2 * width] + pieces[2 * width :]

    seed_group[g] = total_of(n, chosen)
    seeding = exchange("group", lambda d: seed_group.at[d])
    second.wait_recv()
    inverse = factor_inverse(unpack(fold(m, gram_group.at[1])))

    def normalise(image_t):
        embedding = mm(inverse, image_t) * jnp.sqrt(F32(total_rows))
        return embedding / jnp.sqrt(jnp.sum(embedding * embedding, axis=0, keepdims=True) + 1e-06)

    def embed(d):
        unit = normalise(images1[d])
        units[d] = unit
        square[d] = -SHARPNESS * jnp.sum(unit * unit, axis=0, keepdims=True)
        high, low = high_low(unit)
        for at, piece in enumerate((high, low, high)):
            right[d, at * width : (at + 1) * width] = piece
        left[d, :width] = high
        left[d, width : 2 * width] = low

    loop(n, embed)
    unit_copy = pltpu.make_async_copy(units.at[me], unit_out, out_sems.at[0])
    unit_copy.start()
    seeding.wait_recv()
    centres = normalise(fold(m, seed_group))
    for turn in range(KSTEPS):
        high, low = high_low(2.0 * SHARPNESS * centres)
        bias = [v.astype(F32) for v in three(-SHARPNESS * jnp.sum(centres * centres, axis=0, keepdims=True))]
        bias = jnp.concatenate([*bias, jnp.zeros((MASS_ROWS - len(bias), part), F32)], axis=0).astype(jnp.bfloat16)
        table = jnp.concatenate([high, high, low, bias], axis=0)

        def weigh(d):
            values = jnp.exp(dot16(table, right[d], TN) + square[d])
            weights[d] = values
            den[turn, me, pl.ds(d, 1)] = jnp.sum(values, axis=0, keepdims=True)

        loop(n, weigh)
        exchange("dev", lambda d: den.at[turn, d]).wait_recv()
        units_of = 1.0 / fold(n, den.at[turn])
        weights_scale[...] = units_of

        def gathered(d):
            member = weights[d] * weights_scale[pl.ds(d, 1)]
            return dot16(left[d], member.astype(jnp.bfloat16), NT)

        pair = total_of(n, gathered)
        mass = pair[2 * width : 2 * width + 1]
        sums[turn, g, :width] = pair[:width] + pair[width : 2 * width]
        sums[turn, g, width:] = jnp.broadcast_to(mass, (8, part))
        exchange("group", lambda d: sums.at[turn, d]).wait_recv()
        total = fold(m, sums.at[turn])
        centres = total[:width] / total[width : width + 1]
    final[...] = centres.astype(jnp.bfloat16)
    own_copy = pltpu.make_async_copy(final, centres_out.at[me], out_sems.at[1])
    own_copy.start()
    exchange("dev", lambda d: centres_out.at[d], lambda p: final).wait_recv()
    own_copy.wait()
    unit_copy.wait()
    for made in pending:
        made.wait_send()
    gather.wait_send()


def local(tile_values, tile_rows, tile_columns, tile_count, start_basis, seed_rows):
    n, m = lax.axis_size("dev"), lax.axis_size("group")
    slots, block = tile_values.shape[0], tile_values.shape[1]
    local_rows, width = start_basis.shape
    row_blocks = local_rows // block
    clusters = seed_rows.shape[0]
    part = clusters // n
    anywhere = pl.BlockSpec(memory_space=pl.ANY)
    half = (width // 2, 2 * width)
    B16 = jnp.bfloat16
    axes = ["dev", "dev", "dev", "group", "dev", "dev", "dev", "group", "group"]
    axes += ["dev", "group"] * KSTEPS + ["dev"]
    sems = []
    for axis in axes:
        sems += [pltpu.SemaphoreType.DMA((n if axis == "dev" else m,))] * 2
    unit, centres = pl.pallas_call(
        functools.partial(kernel, n, m, local_rows * n * m),
        out_shape=(
            jax.ShapeDtypeStruct((width, local_rows), F32),
            jax.ShapeDtypeStruct((n, width, part), B16),
        ),
        in_specs=[anywhere] * 6,
        out_specs=(anywhere, anywhere),
        scratch_shapes=[
            pltpu.VMEM(tile_values.shape, B16),
            pltpu.SMEM(tile_rows.shape, jnp.int32),
            pltpu.SMEM(tile_columns.shape, jnp.int32),
            pltpu.SMEM((1, 1), jnp.int32),
            pltpu.VMEM((1, part), jnp.int32),
            pltpu.VMEM((local_rows, slots * block), B16),
            pltpu.VMEM((n * row_blocks, width, block), B16),
            pltpu.VMEM((n * row_blocks, width, block), B16),
            pltpu.VMEM((n, width, local_rows), F32),
            pltpu.VMEM((n, width, local_rows), F32),
            pltpu.VMEM((2, n, *half), F32),
            pltpu.VMEM((2, m, *half), F32),
            pltpu.VMEM((n, local_rows, part), B16),
            pltpu.VMEM((m, width, part), F32),
            pltpu.VMEM((n, 3 * width + MASS_ROWS, local_rows), B16),
            pltpu.VMEM((n, 2 * width + MASS_ROWS, local_rows), B16),
            pltpu.VMEM((n, 1, local_rows), F32),
            pltpu.VMEM((n, width, local_rows), F32),
            pltpu.VMEM((n, part, local_rows), F32),
            pltpu.VMEM((KSTEPS, n, n, local_rows), F32),
            pltpu.VMEM((n, local_rows), F32),
            pltpu.VMEM((KSTEPS, m, width + 8, part), F32),
            pltpu.VMEM((width, part), B16),
            pltpu.SemaphoreType.DMA((row_blocks + 5,)),
            pltpu.SemaphoreType.DMA((2,)),
            *sems,
        ],
        compiler_params=pltpu.CompilerParams(
            collective_id=0, has_side_effects=True, vmem_limit_bytes=58 * 1024 * 1024
        ),
        name="spectral",
    )(tile_values, tile_rows, tile_columns, tile_count.reshape(1, 1), start_basis.T, seed_rows.reshape(n, 1, part))
    return unit.T, centres.transpose(0, 2, 1).reshape(clusters, width).astype(F32)


def solution(mesh):
    return jax.shard_map(
        local,
        mesh=mesh,
        in_specs=(
            P(("group", "dev"), None, None),
            P(("group", "dev")),
            P(("group", "dev")),
            P(("group", "dev")),
            P(("group", "dev"), None),
            P(),
        ),
        out_specs=(P(("group", "dev"), None), P()),
        check_vma=False,
    )
```

time: 75.2 us -> 62.1 us (0.83)
  Pallas kernels: 70.6 us -> 58.4 us
  local copies, waits for them, and re-layouts: 3.14 us -> 0.63 us
  other arithmetic: 0 us -> 1.66 us
    pallas_call x1, Pallas kernels: 70.6 us -> 58.4 us  [local(): pl.pallas_call(functools.partial(kernel, n, m, local_rows * n * m), out_s...]
    unnamed x2 -> x3, local copies, waits for them, and re-layouts: 3.14 us -> 0.63 us
    convert_element_type x0 -> x1, other arithmetic: none -> 1.66 us  [local(): centres.transpose(0, 2, 1).reshape(clusters, width).astype(F32)]
where the time goes in v1:
time: 62.1 us; the launch traced here: 62 us
  Pallas kernels  58.4 us (94%)
  other arithmetic  1.66 us (3%)
  between operations  1.29 us (2%)
  local copies, waits for them, and re-layouts  0.63 us (1%)
    pallas_call x1, Pallas kernels, local(): pl.pallas_call(functools.partial(kernel, n, m, local_rows * n * m), out_s...  58.4 us
    convert_element_type x1, other arithmetic, local(): centres.transpose(0, 2, 1).reshape(clusters, width).astype(F32)  1.66 us

profile of v1, /device:TPU:0, one launch (start us, length us, event | category | flops | bytes accessed | tf_op | source)
XLA Modules:
  0.0 62.0 jit_solution(9151375175968011556)
XLA Ops:
  1.3 58.4 %spectral.1 = (f32[64,256]{1,0:T(8,128)}, bf16[8,64,128]{2,1,0:T(8,128)(2,1)}) custom-call(bf16[16,128,128]{2,1,0:T(8,128)(2,1)} %tiles_in.1, s32[16]{0:T(128)} %rows_in.1, s32[16]{0:T(128)} %columns_in.1, s32[1,1]{1,0:T(1,128)} %bitcast.10.count_in, bf16[64,256]{1,0:T(8,128)(2,1)} %bitcast.12, s32[8,1,128]{2,1,0:T(1,128)} %bitcast.13), custom_call_target="tpu_custom_call" | custom-call | tf_op jit(solution)/shard_map/spectral/pallas_call | solution.py:381
  59.7 0.0 copy-start
  59.7 1.7 %copy_bitcast_fusion = f32[1024,64]{0,1:T(8,128)} fusion(bf16[8,64,128]{2,1,0:T(8,128)(2,1)} %get-tuple-element.5), kind=kLoop, calls=%fused_computation | loop fusion | flops 65536 | bytes 393216 | tf_op jit(solution)/shard_map/convert_element_type | solution.py:422
  61.3 0.0 copy-done
  61.3 0.6 %copy.13 = f32[256,64]{0,1:T(8,128)} copy(f32[256,64]{0,1:T(8,128)S(1)} %bitcast.11) | data formatting | bytes 131072
Async XLA Ops:
  59.7 1.7 %copy-start = (f32[64,256]{1,0:T(8,128)S(1)}, f32[64,256]{1,0:T(8,128)}, u32[]{:S(2)}) copy-start(f32[64,256]{1,0:T(8,128)} %get-tuple-element.4) | copy-start | bytes 196612

commit v2 on v1

--- a/solution.py
+++ b/solution.py
@@ -59,6 +59,15 @@
     return lax.fori_loop(1, n, lambda i, total: total + ref[i].astype(F32), total)
 
 
+def flip(me, mask):
+    out, bit = me, 1
+    while bit <= mask:
+        if mask & bit:
+            out = out + bit - 2 * bit * lax.rem(out // bit, 2)
+        bit *= 2
+    return out
+
+
 class Exchange:
     def __init__(self, axis, n, me, land, sems, source=None):
         self.axis, self.n, self.me = axis, n, me
@@ -77,6 +86,8 @@
         )
 
     def peer(self, i):
+        if self.n <= 8 and self.n & (self.n - 1) == 0:
+            return flip(self.me, self.n - 1 - i)
         return lax.rem(self.me + 1 + i, self.n)
 
     def start(self):
@@ -265,12 +276,12 @@
 
     def start_gram(image, turn):
         gram_dev[turn, me] = pack(mm(image, image, NT))
-        return exchange("dev", lambda d: gram_dev.at[turn, d])
+        return exchange("dev", lambda d, turn=turn: gram_dev.at[turn, d])
 
     def end_gram(first, turn):
         first.wait_recv()
         gram_group[turn, g] = fold(n, gram_dev.at[turn])
-        return exchange("group", lambda d: gram_group.at[turn, d])
+        return exchange("group", lambda d, turn=turn: gram_group.at[turn, d])
 
     gather.wait_recv()
     image = apply(basis0)
@@ -305,6 +316,11 @@
     seeding = exchange("group", lambda d: seed_group.at[d])
     second.wait_recv()
     inverse = factor_inverse(unpack(fold(m, gram_group.at[1])))
+
+    def spread(mass):
+        at = lax.broadcasted_iota(jnp.int32, (MASS_ROWS, part), 0)
+        high, low = (v.astype(F32) for v in high_low(mass))
+        return jnp.where(at == 0, high, jnp.where(at == 1, low, 0.0)).astype(jnp.bfloat16)
 
     def normalise(image_t):
         embedding = mm(inverse, image_t) * jnp.sqrt(F32(total_rows))
@@ -337,7 +353,7 @@
             den[turn, me, pl.ds(d, 1)] = jnp.sum(values, axis=0, keepdims=True)
 
         loop(n, weigh)
-        exchange("dev", lambda d: den.at[turn, d]).wait_recv()
+        exchange("dev", lambda d, turn=turn: den.at[turn, d]).wait_recv()
         units_of = 1.0 / fold(n, den.at[turn])
         weights_scale[...] = units_of
 
@@ -347,11 +363,11 @@
 
         pair = total_of(n, gathered)
         mass = pair[2 * width : 2 * width + 1]
-        sums[turn, g, :width] = pair[:width] + pair[width : 2 * width]
-        sums[turn, g, width:] = jnp.broadcast_to(mass, (8, part))
-        exchange("group", lambda d: sums.at[turn, d]).wait_recv()
+        sums[turn, g, :width] = (pair[:width] + pair[width : 2 * width]).astype(jnp.bfloat16)
+        sums[turn, g, width:] = spread(mass)
+        exchange("group", lambda d, turn=turn: sums.at[turn, d]).wait_recv()
         total = fold(m, sums.at[turn])
-        centres = total[:width] / total[width : width + 1]
+        centres = total[:width] / (total[width : width + 1] + total[width + 1 : width + 2])
     final[...] = centres.astype(jnp.bfloat16)
     own_copy = pltpu.make_async_copy(final, centres_out.at[me], out_sems.at[1])
     own_copy.start()
@@ -363,6 +379,11 @@
     gather.wait_send()
 
 
+def widen(n, unit_in, parts, unit_out, centres_out):
+    unit_out[...] = unit_in[...]
+    centres_out[...] = jnp.concatenate([parts[d].astype(F32) for d in range(n)], axis=1)
+
+
 def local(tile_values, tile_rows, tile_columns, tile_count, start_basis, seed_rows):
     n, m = lax.axis_size("dev"), lax.axis_size("group")
     slots, block = tile_values.shape[0], tile_values.shape[1]
@@ -370,6 +391,7 @@
     row_blocks = local_rows // block
     clusters = seed_rows.shape[0]
     part = clusters // n
+    vmem = pl.BlockSpec(memory_space=pltpu.VMEM)
     anywhere = pl.BlockSpec(memory_space=pl.ANY)
     half = (width // 2, 2 * width)
     B16 = jnp.bfloat16
@@ -381,11 +403,11 @@
     unit, centres = pl.pallas_call(
         functools.partial(kernel, n, m, local_rows * n * m),
         out_shape=(
-            jax.ShapeDtypeStruct((width, local_rows), F32),
-            jax.ShapeDtypeStruct((n, width, part), B16),
+            pltpu.VMEM((width, local_rows), F32),
+            pltpu.VMEM((n, width, part), B16),
         ),
         in_specs=[anywhere] * 6,
-        out_specs=(anywhere, anywhere),
+        out_specs=(vmem, vmem),
         scratch_shapes=[
             pltpu.VMEM(tile_values.shape, B16),
             pltpu.SMEM(tile_rows.shape, jnp.int32),
@@ -408,7 +430,7 @@
             pltpu.VMEM((n, part, local_rows), F32),
             pltpu.VMEM((KSTEPS, n, n, local_rows), F32),
             pltpu.VMEM((n, local_rows), F32),
-            pltpu.VMEM((KSTEPS, m, width + 8, part), F32),
+            pltpu.VMEM((KSTEPS, m, width + MASS_ROWS, part), B16),
             pltpu.VMEM((width, part), B16),
             pltpu.SemaphoreType.DMA((row_blocks + 5,)),
             pltpu.SemaphoreType.DMA((2,)),
@@ -419,7 +441,18 @@
         ),
         name="spectral",
     )(tile_values, tile_rows, tile_columns, tile_count.reshape(1, 1), start_basis.T, seed_rows.reshape(n, 1, part))
-    return unit.T, centres.transpose(0, 2, 1).reshape(clusters, width).astype(F32)
+    vmem = pl.BlockSpec(memory_space=pltpu.VMEM)
+    unit, centres = pl.pallas_call(
+        functools.partial(widen, n),
+        out_shape=(
+            jax.ShapeDtypeStruct((width, local_rows), F32),
+            jax.ShapeDtypeStruct((width, clusters), F32),
+        ),
+        in_specs=[vmem, vmem],
+        out_specs=(vmem, vmem),
+        name="widen",
+    )(pltpu.with_memory_space_constraint(unit, pltpu.VMEM), pltpu.with_memory_space_constraint(centres, pltpu.VMEM))
+    return unit.T, centres.T
 
 
 def solution(mesh):

time: 62.1 us -> 57.7 us (0.929)
  Pallas kernels: 58.4 us -> 56.3 us
  other arithmetic: 1.66 us -> 0 us
  local copies, waits for them, and re-layouts: 0.63 us -> 0 us
    pallas_call x1, Pallas kernels: 58.4 us -> 55.6 us  [local(): pl.pallas_call(functools.partial(kernel, n, m, local_rows * n * m), out_s...]
    convert_element_type x1 -> x0, other arithmetic: 1.66 us -> none  [local(): centres.transpose(0, 2, 1).reshape(clusters, width).astype(F32)]
    pallas_call x0 -> x1, Pallas kernels: none -> 0.74 us  [local(): pl.pallas_call(functools.partial(widen, n), out_shape=(jax.ShapeDtypeStru...]
    unnamed x3 -> x0, local copies, waits for them, and re-layouts: 0.63 us -> none
where the time goes in v2:
time: 57.7 us; the launch traced here: 57.6 us
  Pallas kernels  56.3 us (98%)
  between operations  1.28 us (2%)
    pallas_call x1, Pallas kernels, local(): pl.pallas_call(functools.partial(kernel, n, m, local_rows * n * m), out_s...  55.6 us

profile of v2, /device:TPU:0, one launch (start us, length us, event | category | flops | bytes accessed | tf_op | source)
XLA Modules:
  0.0 57.6 jit_solution(14236216299738182077)
XLA Ops:
  1.3 55.6 %spectral.1 = (f32[64,256]{1,0:T(8,128)S(1)}, bf16[8,64,128]{2,1,0:T(8,128)(2,1)S(1)}) custom-call(bf16[16,128,128]{2,1,0:T(8,128)(2,1)} %tiles_in.1, s32[16]{0:T(128)} %rows_in.1, s32[16]{0:T(128)} %columns_in.1, s32[1,1]{1,0:T(1,128)} %bitcast.5.count_in, bf16[64,256]{1,0:T(8,128)(2,1)} %bitcast.6, s32[8,1,128]{2,1,0:T(1,128)} %bitcast.7), custom_call_target="tpu_custom_call" | custom-call | tf_op jit(solution)/shard_map/spectral/pallas_call | solution.py:403
  56.9 0.7 %widen.1 = (f32[64,256]{1,0:T(8,128)}, f32[64,1024]{1,0:T(8,128)}) custom-call(f32[64,256]{1,0:T(8,128)S(1)} %get-tuple-element.6.unit_in, bf16[8,64,128]{2,1,0:T(8,128)(2,1)S(1)} %get-tuple-element.7.parts), custom_call_target="tpu_custom_call" | custom-call | tf_op jit(solution)/shard_map/widen/pallas_call | solution.py:445

commit v3 on v2

--- a/solution.py
+++ b/solution.py
@@ -59,6 +59,10 @@
     return lax.fori_loop(1, n, lambda i, total: total + ref[i].astype(F32), total)
 
 
+def small(n):
+    return n <= 8 and n & (n - 1) == 0
+
+
 def flip(me, mask):
     out, bit = me, 1
     while bit <= mask:
@@ -86,7 +90,7 @@
         )
 
     def peer(self, i):
-        if self.n <= 8 and self.n & (self.n - 1) == 0:
+        if small(self.n):
             return flip(self.me, self.n - 1 - i)
         return lax.rem(self.me + 1 + i, self.n)
 
@@ -127,11 +131,14 @@
         )
 
     def far(self, i):
+        if small(self.n):
+            return flip(self.me, 2 * (i + 1))
         return lax.rem(self.me + 2 + 2 * i, self.n)
 
     def start(self):
         self.copy(self.me, self.me, self.twin, 1).start()
-        loop(self.n // 2 - 1, lambda i: self.copy(self.me, self.far(i), self.far(i), 0).start())
+        last = self.n // 2 - 2
+        loop(last + 1, lambda i: self.copy(self.me, self.far(last - i), self.far(last - i), 0).start())
 
     def relay(self):
         def one(i):
@@ -268,8 +275,6 @@
         right[d, 3 * width :] = jnp.ones((MASS_ROWS, local_rows), jnp.bfloat16)
         left[d, 2 * width :] = jnp.ones((MASS_ROWS, local_rows), jnp.bfloat16)
 
-    loop(n, choose)
-
     def apply(basis):
         picked = jnp.concatenate([basis[columns_ref[s]] for s in range(slots)], axis=1)
         return lax.dot_general(picked, matrix[...], NT, preferred_element_type=F32)
@@ -283,15 +288,18 @@
         gram_group[turn, g] = fold(n, gram_dev.at[turn])
         return exchange("group", lambda d, turn=turn: gram_group.at[turn, d])
 
+    loop(n, choose)
     gather.wait_recv()
     image = apply(basis0)
     first = start_gram(image, 0)
     images0[me] = image
-    gather = exchange("dev", lambda d: images0.at[d])
+    gather0 = Gather(n, me, lambda d: images0.at[d], [next(used) for _ in range(2)])
+    gather0.start()
     second = end_gram(first, 0)
+    gather0.relay()
     second.wait_recv()
     inverse = factor_inverse(unpack(fold(m, gram_group.at[0])))
-    gather.wait_recv()
+    gather0.wait_recv()
 
     def solve(d):
         solved = mm(inverse, images0[d])
@@ -376,6 +384,7 @@
     unit_copy.wait()
     for made in pending:
         made.wait_send()
+    gather0.wait_send()
     gather.wait_send()
 
 
@@ -395,7 +404,7 @@
     anywhere = pl.BlockSpec(memory_space=pl.ANY)
     half = (width // 2, 2 * width)
     B16 = jnp.bfloat16
-    axes = ["dev", "dev", "dev", "group", "dev", "dev", "dev", "group", "group"]
+    axes = ["dev", "dev", "dev", "dev", "group", "dev", "dev", "dev", "group", "group"]
     axes += ["dev", "group"] * KSTEPS + ["dev"]
     sems = []
     for axis in axes:

time: 57.7 us -> 56.5 us (0.979)
  Pallas kernels: 56.3 us -> 55.1 us
    pallas_call x1, Pallas kernels: 55.6 us -> 54.4 us  [local(): pl.pallas_call(functools.partial(kernel, n, m, local_rows * n * m), out_s...]
where the time goes in v3:
time: 56.5 us; the launch traced here: 56.4 us
  Pallas kernels  55.1 us (98%)
  between operations  1.28 us (2%)
    pallas_call x1, Pallas kernels, local(): pl.pallas_call(functools.partial(kernel, n, m, local_rows * n * m), out_s...  54.4 us

profile of v3, /device:TPU:0, one launch (start us, length us, event | category | flops | bytes accessed | tf_op | source)
XLA Modules:
  0.0 56.4 jit_solution(13764180807326517699)
XLA Ops:
  1.3 54.4 %spectral.1 = (f32[64,256]{1,0:T(8,128)S(1)}, bf16[8,64,128]{2,1,0:T(8,128)(2,1)S(1)}) custom-call(bf16[16,128,128]{2,1,0:T(8,128)(2,1)} %tiles_in.1, s32[16]{0:T(128)} %rows_in.1, s32[16]{0:T(128)} %columns_in.1, s32[1,1]{1,0:T(1,128)} %bitcast.5.count_in, bf16[64,256]{1,0:T(8,128)(2,1)} %bitcast.6, s32[8,1,128]{2,1,0:T(1,128)} %bitcast.7), custom_call_target="tpu_custom_call" | custom-call | tf_op jit(solution)/shard_map/spectral/pallas_call | solution.py:412
  55.6 0.7 %widen.1 = (f32[64,256]{1,0:T(8,128)}, f32[64,1024]{1,0:T(8,128)}) custom-call(f32[64,256]{1,0:T(8,128)S(1)} %get-tuple-element.6.unit_in, bf16[8,64,128]{2,1,0:T(8,128)(2,1)S(1)} %get-tuple-element.7.parts), custom_call_target="tpu_custom_call" | custom-call | tf_op jit(solution)/shard_map/widen/pallas_call | solution.py:454

commit v4 on v3

--- a/solution.py
+++ b/solution.py
@@ -261,9 +261,10 @@
     gather = exchange("dev", lambda d: basis0.at[pl.ds(d * row_blocks, row_blocks)])
     count = count_ref[0, 0]
     for s in range(slots):
+        turned = tiles[s].T
         for r in range(row_blocks):
             keep = jnp.logical_and(rows_ref[s] == r, s < count)
-            matrix[r * block : (r + 1) * block, s * block : (s + 1) * block] = tiles[s] * jnp.where(
+            matrix[s * block : (s + 1) * block, r * block : (r + 1) * block] = turned * jnp.where(
                 keep, 1.0, 0.0
             ).astype(jnp.bfloat16)
 
@@ -277,7 +278,7 @@
 
     def apply(basis):
         picked = jnp.concatenate([basis[columns_ref[s]] for s in range(slots)], axis=1)
-        return lax.dot_general(picked, matrix[...], NT, preferred_element_type=F32)
+        return dot16(picked, matrix[...])
 
     def start_gram(image, turn):
         gram_dev[turn, me] = pack(mm(image, image, NT))
@@ -423,7 +424,7 @@
             pltpu.SMEM(tile_columns.shape, jnp.int32),
             pltpu.SMEM((1, 1), jnp.int32),
             pltpu.VMEM((1, part), jnp.int32),
-            pltpu.VMEM((local_rows, slots * block), B16),
+            pltpu.VMEM((slots * block, local_rows), B16),
             pltpu.VMEM((n * row_blocks, width, block), B16),
             pltpu.VMEM((n * row_blocks, width, block), B16),
             pltpu.VMEM((n, width, local_rows), F32),

time: 56.5 us -> 56 us (level)
  Pallas kernels: 55.1 us -> 54.5 us
where the time goes in v4:
time: 56 us; the launch traced here: 55.8 us
  Pallas kernels  54.5 us (97%)
  between operations  1.28 us (2%)
    pallas_call x1, Pallas kernels, local(): pl.pallas_call(functools.partial(kernel, n, m, local_rows * n * m), out_s...  53.8 us

profile of v4, /device:TPU:0, one launch (start us, length us, event | category | flops | bytes accessed | tf_op | source)
XLA Modules:
  0.0 55.8 jit_solution(6211205700101730201)
XLA Ops:
  1.3 53.8 %spectral.1 = (f32[64,256]{1,0:T(8,128)S(1)}, bf16[8,64,128]{2,1,0:T(8,128)(2,1)S(1)}) custom-call(bf16[16,128,128]{2,1,0:T(8,128)(2,1)} %tiles_in.1, s32[16]{0:T(128)} %rows_in.1, s32[16]{0:T(128)} %columns_in.1, s32[1,1]{1,0:T(1,128)} %bitcast.5.count_in, bf16[64,256]{1,0:T(8,128)(2,1)} %bitcast.6, s32[8,1,128]{2,1,0:T(1,128)} %bitcast.7), custom_call_target="tpu_custom_call" | custom-call | tf_op jit(solution)/shard_map/spectral/pallas_call | solution.py:413
  55.1 0.7 %widen.1 = (f32[64,256]{1,0:T(8,128)}, f32[64,1024]{1,0:T(8,128)}) custom-call(f32[64,256]{1,0:T(8,128)S(1)} %get-tuple-element.6.unit_in, bf16[8,64,128]{2,1,0:T(8,128)(2,1)S(1)} %get-tuple-element.7.parts), custom_call_target="tpu_custom_call" | custom-call | tf_op jit(solution)/shard_map/widen/pallas_call | solution.py:455

commit v5 on v4

--- a/solution.py
+++ b/solution.py
@@ -333,7 +333,7 @@
 
     def normalise(image_t):
         embedding = mm(inverse, image_t) * jnp.sqrt(F32(total_rows))
-        return embedding / jnp.sqrt(jnp.sum(embedding * embedding, axis=0, keepdims=True) + 1e-06)
+        return embedding * (1.0 / jnp.sqrt(jnp.sum(embedding * embedding, axis=0, keepdims=True) + 1e-06))
 
     def embed(d):
         unit = normalise(images1[d])
@@ -359,9 +359,10 @@
         def weigh(d):
             values = jnp.exp(dot16(table, right[d], TN) + square[d])
             weights[d] = values
-            den[turn, me, pl.ds(d, 1)] = jnp.sum(values, axis=0, keepdims=True)
+            weights_scale[pl.ds(d, 1)] = jnp.sum(values, axis=0, keepdims=True)
 
         loop(n, weigh)
+        den[turn, me] = weights_scale[...].astype(jnp.bfloat16)
         exchange("dev", lambda d, turn=turn: den.at[turn, d]).wait_recv()
         units_of = 1.0 / fold(n, den.at[turn])
         weights_scale[...] = units_of
@@ -438,7 +439,7 @@
             pltpu.VMEM((n, 1, local_rows), F32),
             pltpu.VMEM((n, width, local_rows), F32),
             pltpu.VMEM((n, part, local_rows), F32),
-            pltpu.VMEM((KSTEPS, n, n, local_rows), F32),
+            pltpu.VMEM((KSTEPS, n, n, local_rows), B16),
             pltpu.VMEM((n, local_rows), F32),
             pltpu.VMEM((KSTEPS, m, width + MASS_ROWS, part), B16),
             pltpu.VMEM((width, part), B16),

time: 56 us -> 55.8 us (level)
  no operation moved by 1% of the time
where the time goes in v5:
time: 55.8 us; the launch traced here: 55.6 us
  Pallas kernels  54.3 us (97%)
  between operations  1.28 us (2%)
    pallas_call x1, Pallas kernels, local(): pl.pallas_call(functools.partial(kernel, n, m, local_rows * n * m), out_s...  53.6 us

profile of v5, /device:TPU:0, one launch (start us, length us, event | category | flops | bytes accessed | tf_op | source)
XLA Modules:
  0.0 55.6 jit_solution(14381545398221437006)
XLA Ops:
  1.3 53.6 %spectral.1 = (f32[64,256]{1,0:T(8,128)S(1)}, bf16[8,64,128]{2,1,0:T(8,128)(2,1)S(1)}) custom-call(bf16[16,128,128]{2,1,0:T(8,128)(2,1)} %tiles_in.1, s32[16]{0:T(128)} %rows_in.1, s32[16]{0:T(128)} %columns_in.1, s32[1,1]{1,0:T(1,128)} %bitcast.5.count_in, bf16[64,256]{1,0:T(8,128)(2,1)} %bitcast.6, s32[8,1,128]{2,1,0:T(1,128)} %bitcast.7), custom_call_target="tpu_custom_call" | custom-call | tf_op jit(solution)/shard_map/spectral/pallas_call | solution.py:414
  54.9 0.7 %widen.1 = (f32[64,256]{1,0:T(8,128)}, f32[64,1024]{1,0:T(8,128)}) custom-call(f32[64,256]{1,0:T(8,128)S(1)} %get-tuple-element.6.unit_in, bf16[8,64,128]{2,1,0:T(8,128)(2,1)S(1)} %get-tuple-element.7.parts), custom_call_target="tpu_custom_call" | custom-call | tf_op jit(solution)/shard_map/widen/pallas_call | solution.py:456

commit v6 on v5

--- a/solution.py
+++ b/solution.py
@@ -197,9 +197,9 @@
         for c, values in column.items():
             for r in range(8):
                 parts[c] = parts[c] - values[r] * (row[r] * over[r])
-        own = row[0] / jnp.sqrt(cell[0][0])
+        own = row[0] * lax.rsqrt(cell[0][0])
         for s in range(1, 8):
-            own = jnp.where(sub == s, row[s] / jnp.sqrt(cell[s][s]), own)
+            own = jnp.where(sub == s, row[s] * lax.rsqrt(cell[s][s]), own)
         done.append(own)
     return jnp.concatenate(done, axis=0)[:, k:]
 
@@ -333,7 +333,7 @@
 
     def normalise(image_t):
         embedding = mm(inverse, image_t) * jnp.sqrt(F32(total_rows))
-        return embedding * (1.0 / jnp.sqrt(jnp.sum(embedding * embedding, axis=0, keepdims=True) + 1e-06))
+        return embedding * lax.rsqrt(jnp.sum(embedding * embedding, axis=0, keepdims=True) + 1e-06)
 
     def embed(d):
         unit = normalise(images1[d])

time: 55.8 us -> 55.6 us (level)
  no operation moved by 1% of the time
where the time goes in v6:
time: 55.6 us; the launch traced here: 55.5 us
  Pallas kernels  54.3 us (98%)
  between operations  1.28 us (2%)
    pallas_call x1, Pallas kernels, local(): pl.pallas_call(functools.partial(kernel, n, m, local_rows * n * m), out_s...  53.5 us

profile of v6, /device:TPU:0, one launch (start us, length us, event | category | flops | bytes accessed | tf_op | source)
XLA Modules:
  0.0 55.5 jit_solution(17572429258760940709)
XLA Ops:
  1.3 53.5 %spectral.1 = (f32[64,256]{1,0:T(8,128)S(1)}, bf16[8,64,128]{2,1,0:T(8,128)(2,1)S(1)}) custom-call(bf16[16,128,128]{2,1,0:T(8,128)(2,1)} %tiles_in.1, s32[16]{0:T(128)} %rows_in.1, s32[16]{0:T(128)} %columns_in.1, s32[1,1]{1,0:T(1,128)} %bitcast.5.count_in, bf16[64,256]{1,0:T(8,128)(2,1)} %bitcast.6, s32[8,1,128]{2,1,0:T(1,128)} %bitcast.7), custom_call_target="tpu_custom_call" | custom-call | tf_op jit(solution)/shard_map/spectral/pallas_call | solution.py:414
  54.8 0.7 %widen.1 = (f32[64,256]{1,0:T(8,128)}, f32[64,1024]{1,0:T(8,128)}) custom-call(f32[64,256]{1,0:T(8,128)S(1)} %get-tuple-element.6.unit_in, bf16[8,64,128]{2,1,0:T(8,128)(2,1)S(1)} %get-tuple-element.7.parts), custom_call_target="tpu_custom_call" | custom-call | tf_op jit(solution)/shard_map/widen/pallas_call | solution.py:456
